TPU v7x, 32 devices: a whole 2x2x4 slice. The times are simulated.
32 devices in a mesh: groups: 2 (over y), row: 4 (over z), col: 4 (over x, core).
Axes of the slice: x: 2, y: 2, z: 4, core: 2. Of those that a mesh axis runs over, the one named last changes fastest.
Arguments:
- tokens: bfloat16 [128, 8192], P(('groups', 'row'), 'col'), parts along dimension 0, may hold values from -6 to 6
- gate_tiles: bfloat16 [256, 4, 12, 128, 256], P(('groups', 'row'), 'col'), parts along dimension 0, may hold values from -0.09375 to 0.09375
- gate_lists: int32 [256, 4, 12], P(('groups', 'row'), 'col'), parts along dimension 0, may hold values from 0 to 15, as said below
- gate_counts: int32 [256, 4], P(('groups', 'row'), 'col'), parts along dimension 0, may hold values from 4 to 12, as said below
- down_tiles: bfloat16 [128, 4, 24, 128, 128], P(('groups', 'row'), 'col'), parts along dimension 0, may hold values from -0.0625 to 0.0625
- down_lists: int32 [128, 4, 24], P(('groups', 'row'), 'col'), parts along dimension 0, may hold values from 0 to 31, as said below
- down_counts: int32 [128, 4], P(('groups', 'row'), 'col'), parts along dimension 0, may hold values from 8 to 24, as said below
Outputs:
- ffn_out: bfloat16 [128, 8192], P(('groups', 'col'), 'row'), parts along dimension 0
There are 2 independent parts, one for each index of `groups`. A program takes and returns all parts, laid end to end along the dimension named above; each array names one. Nothing has to cross between parts.
Inputs may be any that keep to these rules, and one draw needn't show every extreme that they name: `gate_lists`: within each panel the 12 entries are distinct; only the first gate_counts entries are used. `gate_counts`: some panel uses all 12 slots. `down_lists`: within each panel the 24 entries are distinct; only the first down_counts entries are used. `down_counts`: some panel uses all 24 slots.
All inputs are finite; a program needn't handle non-finite values.
Results may differ from a plain program's by a relative error of at most 0.005.
Values may be sent and summed in bfloat16 or wider, within the bound.
No kernel may reach another device: no remote copies, remote signals or barrier semaphores. Data moves between devices by JAX's collectives and lax.ppermute only.
A program may use at most 192 MiB of HBM per device.

v0:
```python
import jax
import jax.numpy as jnp
from jax import lax
from jax.sharding import PartitionSpec as P


def slot_mask(slot_counts, slot_total):
    slots = jnp.arange(slot_total, dtype=jnp.int32)
    return (slots < slot_counts[..., None]).astype(jnp.bfloat16)


def local(tokens, gate_tiles, gate_lists, gate_counts, down_tiles, down_lists, down_counts):
    block = gate_tiles.shape[3]
    columns = lax.axis_size("col")
    local_hidden = gate_tiles.shape[0]
    all_tokens = lax.all_gather(tokens, "row", axis=0, tiled=True)
    total_rows = all_tokens.shape[0]
    quarter = total_rows // columns
    lists_here = gate_lists[:, 0, :]
    keep_gate = slot_mask(gate_counts[:, 0], gate_lists.shape[2])
    tiles_here = gate_tiles[:, 0]
    row_count = all_tokens.shape[0]
    blocks_grid = all_tokens.reshape(row_count, -1, block)
    chosen = blocks_grid[:, lists_here, :] * keep_gate[None, :, :, None]
    product = jnp.einsum("rhsk,hskc->rhc", chosen, tiles_here, preferred_element_type=jnp.float32)
    summed = lax.psum(product.reshape(row_count, -1), "col")
    own_rows = lax.dynamic_slice_in_dim(summed, lax.axis_index("col") * quarter, quarter, 0)
    paired = own_rows.reshape(quarter, local_hidden, 2, block)
    hidden = (
        (jax.nn.silu(paired[:, :, 0]) * paired[:, :, 1]).astype(jnp.bfloat16).reshape(quarter, -1)
    )
    hidden_all = lax.all_gather(hidden, "row", axis=1, tiled=True)
    hidden_width = hidden_all.shape[1]
    quarter_blocks = hidden_width // (block * columns)
    tiles_all = lax.all_gather(down_tiles, "col", axis=1, tiled=True)
    lists_all, counts_all = (
        lax.all_gather(down_lists, "col", axis=1, tiled=True),
        lax.all_gather(down_counts, "col", axis=1, tiled=True),
    )
    offsets = (jnp.arange(columns, dtype=jnp.int32) * quarter_blocks)[None, :, None]
    block_index = lists_all + offsets
    keep_down = slot_mask(counts_all, lists_all.shape[2])
    blocks_grid = hidden_all.reshape(quarter, -1, block)
    chosen = blocks_grid[:, block_index, :] * keep_down[None, :, :, :, None]
    product = jnp.einsum("tdqsk,dqskc->tdc", chosen, tiles_all, preferred_element_type=jnp.float32)
    result = product.reshape(quarter, -1)
    return result.astype(jnp.bfloat16)


def solution(mesh):
    return jax.shard_map(
        local,
        mesh=mesh,
        in_specs=(
            P(("groups", "row"), "col"),
            P(("groups", "row"), "col", None, None, None),
            P(("groups", "row"), "col", None),
            P(("groups", "row"), "col"),
            P(("groups", "row"), "col", None, None, None),
            P(("groups", "row"), "col", None),
            P(("groups", "row"), "col"),
        ),
        out_specs=P(("groups", "col"), "row"),
        check_vma=False,
    )
```

profile of v0, /device:TPU:0, one launch (start us, length us, event | category | flops | bytes accessed | tf_op | source)
XLA Modules:
  0.0 430.9 jit_solution(15397803045704059399)
XLA Ops:
  6.5 0.0 all-reduce.2.cloned.1.call-start
  6.5 15.8 %all_gather.15 = bf16[64,2048]{1,0:T(8,128)(2,1)S(1)} all-gather(bf16[16,2048]{1,0:T(8,128)(2,1)} %param.7), channel_id=1, replica_groups=mesh['groups'=2,'row'=4,'col'=4] {'row'}, dimensions={0}, use_global_device_ids=true | all-gather | bytes 327680 | tf_op jit(solution)/shard_map/all_gather | solution.py:16
  22.4 0.1 copy_bitcast_fusion.1
  22.4 0.7 compare_select_fusion.1
  23.1 0.1 copy.36
  23.2 0.1 reshape.84
  23.3 0.7 fusion.27
  24.1 13.3 %gather_fusion = bf16[384,64,128]{2,1,0:T(8,128)(2,1)} fusion(bf16[64,16,128]{2,0,1:T(8,128)(2,1)S(1)} %copy_bitcast_fusion.1, s32[1024]{0:T(1024)S(1)} %pad_clamp_fusion.1), kind=kCustom, calls=%fused_computation | custom fusion | bytes 12584448 | tf_op jit(solution)/shard_map/gather | solution.py:24
  37.4 12.6 %fusion.8 = f32[32,8,8,256]{3,2,1,0:T(8,128)S(1)} fusion(bf16[32,1,12,128,256]{4,3,2,1,0:T(8,128)(2,1)} %param.8, bf16[32,12,64,128]{3,2,1,0:T(8,128)(2,1)} %bitcast.83, bf16[32,12]{1,0:T(8,128)(2,1)S(1)} %fusion.27), kind=kOutput, calls=%fused_computation.11 | convolution fusion | flops 1613758464 | bytes 33555200 | tf_op jit(solution)/shard_map/rhsk,hskc->rhc/dot_general | solution.py:25
  50.0 1.5 copy.49
  51.5 0.0 all-reduce.2.cloned.1.call-update
  51.6 0.0 all-gather.3.cloned.1.call-start
  51.6 0.0 copy-start
  51.6 0.0 copy-start.1
  51.6 0.7 all-gather.3.cloned.1.call-update
  52.3 0.0 copy-done
  52.3 5.2 %all_gather.17 = s32[16,4,24]{2,0,1:T(8,128)S(1)} all-gather(s32[16,1,24]{2,0,1:T(8,128)S(1)} %bitcast.89), channel_id=1, replica_groups=mesh['groups'=2,'row'=4,'col'=4] {'col'}, dimensions={1}, use_global_device_ids=true | all-gather | bytes 7680 | tf_op jit(solution)/shard_map/all_gather | solution.py:37
  57.5 0.1 compare_select_fusion
  57.6 0.1 reshape.92
  57.7 0.0 copy-done.1
  57.7 5.0 %all-gather = s32[4,1,16]{2,1,0:T(1,128)S(1)} all-gather(s32[1,1,16]{2,1,0:T(1,128)S(1)} %bitcast.92), channel_id=1, replica_groups=mesh['groups'=2,'row'=4,'col'=4] {'col'}, dimensions={0}, use_global_device_ids=true | all-gather | bytes 320 | tf_op jit(solution)/shard_map/all_gather | solution.py:38
  62.8 0.1 fusion.26
  62.9 41.8 %all-reduce.2.cloned.1.call-done = f32[64,8192]{1,0:T(8,128)} async-done(((f32[64,8192]{1,0:T(8,128)}), f32[64,8192]{1,0:T(8,128)}) %all-reduce.2.cloned.1.call-update) | async-done | bytes 2097168 | tf_op jit(solution)/shard_map/psum | solution.py:26
  104.7 1.1 constant_dynamic-slice_fusion
  105.7 0.4 reshape.80
  106.2 1.3 slice_reduce_fusion.1
  107.5 0.3 fusion.22
  107.9 15.7 %all_gather.16 = bf16[16,16384]{1,0:T(8,128)(2,1)S(1)} all-gather(bf16[16,4096]{1,0:T(8,128)(2,1)S(1)} %fusion.22), channel_id=1, replica_groups=mesh['groups'=2,'row'=4,'col'=4] {'row'}, dimensions={1}, use_global_device_ids=true | all-gather | bytes 655360 | tf_op jit(solution)/shard_map/all_gather | solution.py:32
  123.5 0.1 copy_bitcast_fusion
  123.6 5.7 %gather_fusion.1 = bf16[1536,16,128]{2,1,0:T(8,128)(2,1)} fusion(bf16[16,128,128]{2,0,1:T(8,128)(2,1)S(1)} %copy_bitcast_fusion, s32[2048]{0:T(1024)S(1)} %pad_clamp_fusion), kind=kCustom, calls=%fused_computation.1 | custom fusion | bytes 12589056 | tf_op jit(solution)/shard_map/gather | solution.py:44
  129.3 274.2 %all-gather.3.cloned.1.call-done = bf16[16,4,24,128,128]{4,3,2,0,1:T(8,128)(2,1)} async-done(((bf16[16,1,24,128,128]{4,3,2,0,1:T(8,128)(2,1)}), bf16[16,4,24,128,128]{4,3,2,0,1:T(8,128)(2,1)}) %all-gather.3.cloned.1.call-update) | async-done | bytes 50331664 | tf_op jit(solution)/shard_map/all_gather | solution.py:35
  403.5 19.9 %fusion.19 = bf16[16,2,8,128]{3,2,1,0:T(8,128)(2,1)S(1)} fusion(bf16[16,4,24,128,128]{4,3,2,0,1:T(8,128)(2,1)} %all-gather.3.cloned.1.call-done, bf16[16,4,24,16,128]{4,3,2,1,0:T(8,128)(2,1)} %bitcast.84, bf16[16,4,24]{2,0,1:T(8,128)(2,1)S(1)} %fusion.26), kind=kOutput, calls=%fused_computation.14 | convolution fusion | flops 808484864 | bytes 56691712 | tf_op jit(solution)/shard_map/tdqsk,dqskc->tdc/dot_general | solution.py:45
  423.5 0.6 copy.68
  (4 shorter events, 0.0 us)
Async XLA Ops:
  6.5 98.1 %all-reduce.2.cloned.1.call-start = ((), (), s32[]{:S(2)}) async-start(), calls=%async_computation | async-start | bytes 4194304 | tf_op jit(solution)/shard_map/psum | solution.py:26
  51.6 352.0 %all-gather.3.cloned.1.call-start = ((), (), s32[]{:S(2)}) async-start(), calls=%async_computation.1 | async-start | bytes 62914560 | tf_op jit(solution)/shard_map/all_gather | solution.py:35
  51.6 0.7 copy-start
  51.6 6.1 %copy-start.1 = (s32[16,1]{0,1:T(1,128)S(1)}, s32[16,1]{0,1:T(1,128)}, u32[]{:S(2)}) copy-start(s32[16,1]{0,1:T(1,128)} %param.13) | copy-start | bytes 196
Sparse Core Ops, SparseCore 0:
  51.7 52.9 all-reduce.1
  106.3 297.1 all-gather.2
where the time goes:
time: 431 us
  waiting for transfers between devices  317 us (74%)
  blocking collectives  41.7 us (10%)
  matrix products  32.5 us (8%)
  local copies, waits for them, and re-layouts  24.5 us (6%)
  between operations  13.5 us (3%)
    all_gather x1, waiting for transfers between devices, local(): tiles_all = lax.all_gather(down_tiles, 'col', axis=1, tiled=True)  274 us
    psum x1, waiting for transfers between devices, local(): summed = lax.psum(product.reshape(row_count, -1), 'col')  41.8 us
    dot_general x1, matrix products, local(): jnp.einsum('tdqsk,dqskc->tdc', chosen, tiles_all, preferred_element_type=...  19.9 us
    all_gather x1, blocking collectives, local(): all_tokens = lax.all_gather(tokens, 'row', axis=0, tiled=True)  15.8 us
    all_gather x1, blocking collectives, local(): hidden_all = lax.all_gather(hidden, 'row', axis=1, tiled=True)  15.7 us
    gather x1, local copies, waits for them, and re-layouts, local(): chosen = blocks_grid[:, lists_here, :] * keep_gate[None, :, :, None]  13.3 us
    dot_general x1, matrix products, local(): jnp.einsum('rhsk,hskc->rhc', chosen, tiles_here, preferred_element_type=j...  12.6 us
  transfers between devices with their start and end apart: 2, of which 2 were waited for; matrix products, arithmetic and copies ran while one was open for 2% of the time, Pallas kernels for 0%

commit v1 on v0

--- a/solution.py
+++ b/solution.py
@@ -13,7 +13,12 @@
     block = gate_tiles.shape[3]
     columns = lax.axis_size("col")
     local_hidden = gate_tiles.shape[0]
-    all_tokens = lax.all_gather(tokens, "row", axis=0, tiled=True)
+    ring = [tokens]
+    for hop in range(3):
+        ring.append(lax.ppermute(ring[-1], "row", [(dev, (dev + 1) % 4) for dev in range(4)]))
+    all_tokens = jnp.roll(
+        jnp.concatenate(ring[::-1], axis=0), (lax.axis_index("row") + 1) * ring[0].shape[0], axis=0
+    )
     total_rows = all_tokens.shape[0]
     quarter = total_rows // columns
     lists_here = gate_lists[:, 0, :]

time: 431 us -> 432 us (level)
  blocking collectives: 41.7 us -> 25.9 us
  waiting for transfers between devices: 317 us -> 329 us
    all_gather x1 -> x0, blocking collectives: 15.8 us -> none  [local(): all_tokens = lax.all_gather(tokens, 'row', axis=0, tiled=True)]
    ppermute x0 -> x3, waiting for transfers between devices: none -> 15 us  [local(): lax.ppermute(ring[-1], 'row', [(dev, (dev + 1) % 4) for dev in range(4)])]
  transfers between devices with their start and end apart: 2 -> 5, of which waited for: 2 -> 5; matrix products, arithmetic and copies ran while one was open for 2% -> 3% of each run, Pallas kernels for 0% -> 0%
where the time goes in v1:
time: 432 us
  waiting for transfers between devices  329 us (76%)
  matrix products  32.5 us (8%)
  local copies, waits for them, and re-layouts  26.2 us (6%)
  blocking collectives  25.9 us (6%)
  between operations  13.6 us (3%)
    all_gather x1, waiting for transfers between devices, local(): tiles_all = lax.all_gather(down_tiles, 'col', axis=1, tiled=True)  274 us
    psum x1, waiting for transfers between devices, local(): summed = lax.psum(product.reshape(row_count, -1), 'col')  38.7 us
    dot_general x1, matrix products, local(): jnp.einsum('tdqsk,dqskc->tdc', chosen, tiles_all, preferred_element_type=...  19.9 us
    all_gather x1, blocking collectives, local(): hidden_all = lax.all_gather(hidden, 'row', axis=1, tiled=True)  15.7 us
    ppermute x3, waiting for transfers between devices, local(): lax.ppermute(ring[-1], 'row', [(dev, (dev + 1) % 4) for dev in range(4)])  15 us
    gather x1, local copies, waits for them, and re-layouts, local(): chosen = blocks_grid[:, lists_here, :] * keep_gate[None, :, :, None]  13.3 us
    dot_general x1, matrix products, local(): jnp.einsum('rhsk,hskc->rhc', chosen, tiles_here, preferred_element_type=j...  12.6 us
  transfers between devices with their start and end apart: 5, of which 5 were waited for; matrix products, arithmetic and copies ran while one was open for 3% of the time, Pallas kernels for 0%

profile of v1, /device:TPU:0, one launch (start us, length us, event | category | flops | bytes accessed | tf_op | source)
XLA Modules:
  0.0 431.8 jit_solution(2324533306513782068)
XLA Ops:
  6.5 0.0 all-reduce.2.cloned.1.call-start
  6.5 3.0 collective-permute-start
  9.6 0.7 compare_select_fusion.1
  10.3 3.8 collective-permute-done
  14.0 0.0 collective-permute-start.1
  14.0 0.7 fusion.27
  14.8 0.1 copy.35
  14.9 0.1 reshape.84
  15.0 5.1 %collective-permute-done.1 = bf16[16,2048]{1,0:T(8,128)(2,1)S(1)} collective-permute-done((bf16[16,2048]{1,0:T(8,128)(2,1)S(1)}, bf16[16,2048]{1,0:T(8,128)(2,1)S(1)}, u32[]{:S(2)}, u32[]{:S(2)}) %collective-permute-start.1) | collective-permute-done | bytes 65568 | tf_op jit(solution)/shard_map/ppermute | solution.py:18
  20.1 0.0 collective-permute-start.2
  20.1 6.1 %collective-permute-done.2 = bf16[16,2048]{1,0:T(8,128)(2,1)S(1)} collective-permute-done((bf16[16,2048]{1,0:T(8,128)(2,1)S(1)}, bf16[16,2048]{1,0:T(8,128)(2,1)S(1)}, u32[]{:S(2)}, u32[]{:S(2)}) %collective-permute-start.2) | collective-permute-done | bytes 65568 | tf_op jit(solution)/shard_map/ppermute | solution.py:18
  26.2 0.8 constant_dynamic-update-slice_fusion.4
  27.1 0.8 constant_dynamic-update-slice_fusion
  27.9 0.1 copy_bitcast_fusion.1
  28.0 13.3 %gather_fusion = bf16[384,64,128]{2,1,0:T(8,128)(2,1)} fusion(bf16[64,16,128]{2,0,1:T(8,128)(2,1)S(1)} %copy_bitcast_fusion.1, s32[1024]{0:T(1024)S(1)} %pad_clamp_fusion.1), kind=kCustom, calls=%fused_computation | custom fusion | bytes 12584448 | tf_op jit(solution)/shard_map/gather | solution.py:29
  41.3 12.6 %fusion.8 = f32[32,8,8,256]{3,2,1,0:T(8,128)S(1)} fusion(bf16[32,1,12,128,256]{4,3,2,1,0:T(8,128)(2,1)} %param.8, bf16[32,12,64,128]{3,2,1,0:T(8,128)(2,1)} %bitcast.83, bf16[32,12]{1,0:T(8,128)(2,1)S(1)} %fusion.27), kind=kOutput, calls=%fused_computation.11 | convolution fusion | flops 1613758464 | bytes 33555200 | tf_op jit(solution)/shard_map/rhsk,hskc->rhc/dot_general | solution.py:30
  53.9 1.5 copy.48
  55.5 0.0 all-reduce.2.cloned.1.call-update
  55.5 0.0 all-gather.3.cloned.1.call-start
  55.5 0.0 copy-start
  55.6 0.0 copy-start.1
  55.6 0.7 all-gather.3.cloned.1.call-update
  56.3 0.0 copy-done
  56.3 5.2 %all_gather.13 = s32[16,4,24]{2,0,1:T(8,128)S(1)} all-gather(s32[16,1,24]{2,0,1:T(8,128)S(1)} %bitcast.89), channel_id=1, replica_groups=mesh['groups'=2,'row'=4,'col'=4] {'col'}, dimensions={1}, use_global_device_ids=true | all-gather | bytes 7680 | tf_op jit(solution)/shard_map/all_gather | solution.py:42
  61.5 0.1 compare_select_fusion
  61.6 0.1 reshape.92
  61.7 0.0 copy-done.1
  61.7 5.0 %all-gather = s32[4,1,16]{2,1,0:T(1,128)S(1)} all-gather(s32[1,1,16]{2,1,0:T(1,128)S(1)} %bitcast.92), channel_id=1, replica_groups=mesh['groups'=2,'row'=4,'col'=4] {'col'}, dimensions={0}, use_global_device_ids=true | all-gather | bytes 320 | tf_op jit(solution)/shard_map/all_gather | solution.py:43
  66.7 0.1 fusion.26
  66.8 38.7 %all-reduce.2.cloned.1.call-done = f32[64,8192]{1,0:T(8,128)} async-done(((f32[64,8192]{1,0:T(8,128)}), f32[64,8192]{1,0:T(8,128)}) %all-reduce.2.cloned.1.call-update) | async-done | bytes 2097168 | tf_op jit(solution)/shard_map/psum | solution.py:31
  105.5 1.1 constant_dynamic-slice_fusion
  106.5 0.4 reshape.80
  107.0 1.3 slice_reduce_fusion.1
  108.3 0.3 fusion.22
  108.7 15.7 %all_gather.12 = bf16[16,16384]{1,0:T(8,128)(2,1)S(1)} all-gather(bf16[16,4096]{1,0:T(8,128)(2,1)S(1)} %fusion.22), channel_id=1, replica_groups=mesh['groups'=2,'row'=4,'col'=4] {'row'}, dimensions={1}, use_global_device_ids=true | all-gather | bytes 655360 | tf_op jit(solution)/shard_map/all_gather | solution.py:37
  124.3 0.1 copy_bitcast_fusion
  124.4 5.7 %gather_fusion.1 = bf16[1536,16,128]{2,1,0:T(8,128)(2,1)} fusion(bf16[16,128,128]{2,0,1:T(8,128)(2,1)S(1)} %copy_bitcast_fusion, s32[2048]{0:T(1024)S(1)} %pad_clamp_fusion), kind=kCustom, calls=%fused_computation.1 | custom fusion | bytes 12589056 | tf_op jit(solution)/shard_map/gather | solution.py:49
  130.1 274.2 %all-gather.3.cloned.1.call-done = bf16[16,4,24,128,128]{4,3,2,0,1:T(8,128)(2,1)} async-done(((bf16[16,1,24,128,128]{4,3,2,0,1:T(8,128)(2,1)}), bf16[16,4,24,128,128]{4,3,2,0,1:T(8,128)(2,1)}) %all-gather.3.cloned.1.call-update) | async-done | bytes 50331664 | tf_op jit(solution)/shard_map/all_gather | solution.py:40
  404.4 19.9 %fusion.19 = bf16[16,2,8,128]{3,2,1,0:T(8,128)(2,1)S(1)} fusion(bf16[16,4,24,128,128]{4,3,2,0,1:T(8,128)(2,1)} %all-gather.3.cloned.1.call-done, bf16[16,4,24,16,128]{4,3,2,1,0:T(8,128)(2,1)} %bitcast.84, bf16[16,4,24]{2,0,1:T(8,128)(2,1)S(1)} %fusion.26), kind=kOutput, calls=%fused_computation.14 | convolution fusion | flops 808484864 | bytes 56691712 | tf_op jit(solution)/shard_map/tdqsk,dqskc->tdc/dot_general | solution.py:50
  424.3 0.6 copy.67
  (10 shorter events, 0.1 us)
Async XLA Ops:
  6.5 98.9 %all-reduce.2.cloned.1.call-start = ((), (), s32[]{:S(2)}) async-start(), calls=%async_computation | async-start | bytes 4194304 | tf_op jit(solution)/shard_map/psum | solution.py:31
  6.5 7.5 %collective-permute-start = (bf16[16,2048]{1,0:T(8,128)(2,1)}, bf16[16,2048]{1,0:T(8,128)(2,1)S(1)}, u32[]{:S(2)}, u32[]{:S(2)}) collective-permute-start(bf16[16,2048]{1,0:T(8,128)(2,1)} %param.7), channel_id=1, source_target_pairs={{0,4},{4,8},{8,12},{12,0},{1,5},{5,9},{9,13},{13,1},{2,6},{6,10},{... | collective-permute-start | bytes 196616 | tf_op jit(solution)/shard_map/ppermute | solution.py:18
  14.0 6.1 %collective-permute-start.1 = (bf16[16,2048]{1,0:T(8,128)(2,1)S(1)}, bf16[16,2048]{1,0:T(8,128)(2,1)S(1)}, u32[]{:S(2)}, u32[]{:S(2)}) collective-permute-start(bf16[16,2048]{1,0:T(8,128)(2,1)S(1)} %collective-permute-done), channel_id=1, source_target_pairs={{0,4},{4,8},{8,12},{12,0},{1,5},{5,9},{9,13},{13,1},{2,6},{6,10},{... | collective-permute-start | bytes 196616 | tf_op jit(solution)/shard_map/ppermute | solution.py:18
  20.1 6.1 %collective-permute-start.2 = (bf16[16,2048]{1,0:T(8,128)(2,1)S(1)}, bf16[16,2048]{1,0:T(8,128)(2,1)S(1)}, u32[]{:S(2)}, u32[]{:S(2)}) collective-permute-start(bf16[16,2048]{1,0:T(8,128)(2,1)S(1)} %collective-permute-done.1), channel_id=1, source_target_pairs={{0,4},{4,8},{8,12},{12,0},{1,5},{5,9},{9,13},{13,1},{2,6},{6,10},{... | collective-permute-start | bytes 196616 | tf_op jit(solution)/shard_map/ppermute | solution.py:18
  55.5 348.9 %all-gather.3.cloned.1.call-start = ((), (), s32[]{:S(2)}) async-start(), calls=%async_computation.1 | async-start | bytes 62914560 | tf_op jit(solution)/shard_map/all_gather | solution.py:40
  55.5 0.7 copy-start
  55.6 6.1 %copy-start.1 = (s32[16,1]{0,1:T(1,128)S(1)}, s32[16,1]{0,1:T(1,128)}, u32[]{:S(2)}) copy-start(s32[16,1]{0,1:T(1,128)} %param.13) | copy-start | bytes 196
Sparse Core Ops, SparseCore 0:
  55.6 49.8 all-reduce.1
  107.1 297.1 all-gather.2
